TPU v7x, 32 devices: a whole 2x2x4 slice. The times are simulated.
32 devices in a mesh: groups: 2 (over y), feat: 4 (over z), pts: 2 (over x), sub: 2 (over core).
Axes of the slice: x: 2, y: 2, z: 4, core: 2. Of those that a mesh axis runs over, the one named last changes fastest.
Arguments:
- points: bfloat16 [256, 256], P(('groups', 'pts')), parts along dimension 0, may hold values from -6 to 6
- freqs: bfloat16 [256, 65536], P(None, ('feat', 'sub')), may hold values from -0.75 to 0.75
- phases: float32 [65536], P(('feat', 'sub')), may hold values from 0 to 6.283
- basis: bfloat16 [131072, 1024], P(('groups', 'feat', 'sub'), 'pts'), parts along dimension 0, may hold values from -0.0203125 to 0.0203125
Outputs:
- coefs: float32 [2048, 128], P('groups', 'pts'), parts along dimension 0
- new_basis: float32 [131072, 128], P(('groups', 'feat', 'sub'), 'pts'), parts along dimension 0
- factor: float32 [256, 128], P(('groups', 'pts')), parts along dimension 0
There are 2 independent parts, one for each index of `groups`. A program takes and returns all parts, laid end to end along the dimension named above; an argument that names none is the same for every part. Nothing has to cross between parts.
All inputs are finite; a program needn't handle non-finite values.
Results may differ from a plain program's by a relative error of at most 0.00055.
Values may be sent and summed in bfloat16 or wider, within the bound.
No kernel may reach another device: no remote copies, remote signals or barrier semaphores. Data moves between devices by JAX's collectives and lax.ppermute only.
A program may use at most 128 MiB of HBM per device.

v0:
```python
import jax
import jax.numpy as jnp
from jax import lax
from jax.sharding import PartitionSpec as P

FEATS = 65536


def on_device(points, freqs, phases, basis):
    highest = lax.Precision.HIGHEST
    phase_in = jnp.einsum("pd,df->fp", points, freqs, preferred_element_type=jnp.float32)
    features = jnp.cos(phase_in + phases[:, None])
    point_cols = features.shape[1]
    whole_basis = lax.all_gather(basis, "pts", axis=1, tiled=True).astype(jnp.float32)
    partial_value = jnp.einsum("fk,fp->kp", whole_basis, features, precision=highest)
    coefs = lax.psum(partial_value, ("feat", "sub"))
    fitted = jnp.dot(whole_basis, coefs, precision=highest)
    residual = features - fitted
    spread = lax.all_gather(residual, "pts", axis=1, tiled=True)
    block = jnp.einsum("fq,fp->qp", spread, residual, precision=highest)
    total_pts = block.shape[0]
    block = lax.psum(block, ("feat", "sub")) / FEATS
    gram = lax.all_gather(block, "pts", axis=1, tiled=True)
    factor = jnp.linalg.cholesky(gram)
    eye_mat = jnp.eye(total_pts, dtype=jnp.float32)
    inverse = jax.scipy.linalg.solve_triangular(factor, eye_mat, lower=True)
    offset = lax.axis_index("pts") * point_cols
    factor_rows = lax.dynamic_slice_in_dim(factor, offset, point_cols, 0)
    inv_rows = lax.dynamic_slice_in_dim(inverse, offset, point_cols, 0)
    new_basis = jnp.einsum("fq,pq->fp", spread, inv_rows, precision=highest)
    return (coefs, new_basis, factor_rows)


def solution(mesh):
    return jax.shard_map(
        on_device,
        mesh=mesh,
        in_specs=(
            P(("groups", "pts"), None),
            P(None, ("feat", "sub")),
            P(("feat", "sub")),
            P(("groups", "feat", "sub"), "pts"),
        ),
        out_specs=(
            P("groups", "pts"),
            P(("groups", "feat", "sub"), "pts"),
            P(("groups", "pts"), None),
        ),
        check_vma=False,
    )
```

profile of v0, /device:TPU:0, one launch (start us, length us, event | category | flops | bytes accessed | tf_op | source)
XLA Modules:
  0.0 432.8 jit_solution(4371246499104111773)
XLA Ops:
  7.2 0.0 copy-start
  7.2 0.0 copy-start.2
  7.2 0.0 all-gather.3.cloned.1.call-start
  7.2 0.7 all-gather.3.cloned.1.call-update
  7.9 0.0 all-reduce.2.cloned.1.call-start
  8.0 0.0 copy-done
  8.0 0.0 copy-done.2
  8.0 8.7 %fusion = f32[8192,64]{0,1:T(8,128)S(1)} fusion(bf16[64,256]{1,0:T(8,128)(2,1)S(1)} %copy-done, bf16[256,8192]{1,0:T(8,128)(2,1)} %param.5, f32[8192]{0:T(1024)S(1)} %copy-done.2), kind=kOutput, calls=%fused_computation.1 | convolution fusion | flops 268959744 | bytes 6356992 | tf_op jit(solution)/shard_map/pd,df->fp/dot_general | solution.py:11
  16.7 194.4 %all-gather.3.cloned.1.call-done = bf16[8192,1024]{1,0:T(8,128)(2,1)} async-done(((bf16[8192,512]{1,0:T(8,128)(2,1)}), bf16[8192,1024]{1,0:T(8,128)(2,1)}) %all-gather.3.cloned.1.call-update) | async-done | bytes 16777232 | tf_op jit(solution)/shard_map/all_gather | solution.py:14
  211.2 13.1 %convolution_bitcast_fusion.1 = f32[1024,64]{0,1:T(8,128)} fusion(f32[8192,64]{0,1:T(8,128)S(1)} %fusion, bf16[8192,1024]{1,0:T(8,128)(2,1)} %all-gather.3.cloned.1.call-done), kind=kOutput, calls=%fused_computation.4 | convolution fusion | flops 6442450944 | bytes 19136512 | tf_op jit(solution)/shard_map/fk,fp->kp/dot_general | solution.py:15
  224.3 0.0 all-reduce.2.cloned.1.call-update
  224.3 0.2 all-gather.5.cloned.1.call-start
  224.5 54.8 %all-reduce.2.cloned.1.call-done = f32[1024,64]{0,1:T(8,128)} async-done(((f32[1024,64]{0,1:T(8,128)}), f32[1024,64]{0,1:T(8,128)}) %all-reduce.2.cloned.1.call-update) | async-done | bytes 262160 | tf_op jit(solution)/shard_map/psum | solution.py:16
  279.4 19.7 %fusion.1 = f32[8192,64]{0,1:T(8,128)} fusion(f32[8192,64]{0,1:T(8,128)S(1)} %fusion, f32[1024,64]{0,1:T(8,128)} %all-reduce.2.cloned.1.call-done, bf16[8192,1024]{1,0:T(8,128)(2,1)} %all-gather.3.cloned.1.call-done), kind=kOutput, calls=%fused_computation.3 | convolution fusion | flops 6442975232 | bytes 21233664 | tf_op jit(solution)/shard_map/dot_general | solution.py:17
  299.1 0.0 all-gather.5.cloned.1.call-update
  299.1 55.9 %all-gather.5.cloned.1.call-done = f32[8192,128]{0,1:T(8,128)} async-done(((f32[8192,64]{0,1:T(8,128)}), f32[8192,128]{0,1:T(8,128)}) %all-gather.5.cloned.1.call-update) | async-done | bytes 4194320 | tf_op jit(solution)/shard_map/all_gather | solution.py:19
  355.0 7.3 %fusion.8 = f32[128,64]{0,1:T(8,128)S(1)} fusion(f32[8192,128]{0,1:T(8,128)} %all-gather.5.cloned.1.call-done, f32[8192,64]{0,1:T(8,128)} %fusion.1), kind=kOutput, calls=%fused_computation.20 | convolution fusion | flops 805306368 | bytes 6324224 | tf_op jit(solution)/shard_map/fq,fp->qp/dot_general | solution.py:20
  362.3 0.0 copy-start.1
  362.3 28.7 %psum.15 = f32[128,64]{0,1:T(8,128)S(1)} all-reduce(f32[128,64]{0,1:T(8,128)S(1)} %fusion.8), channel_id=1, replica_groups=mesh['groups'=2,'feat'=4,'pts'=2,'sub'=2] {'feat','sub'}, use_global_device_ids=true, to_apply=%region_1.0 | all-reduce | flops 8192 | bytes 65536 | tf_op jit(solution)/shard_map/psum | solution.py:22
  391.0 4.8 %all_gather.11 = f32[128,128]{0,1:T(8,128)S(1)} all-gather(f32[128,64]{0,1:T(8,128)S(1)} %broadcast_multiply_fusion), channel_id=1, replica_groups=mesh['groups'=2,'feat'=4,'pts'=2,'sub'=2] {'pts'}, dimensions={1}, use_global_device_ids=true | all-gather | bytes 98304 | tf_op jit(solution)/shard_map/all_gather | solution.py:23
  395.8 0.1 copy.7
  395.9 11.7 %cholesky.17 = f32[128,128]{1,0:T(8,128)S(1)} custom-call(f32[128,128]{1,0:T(8,128)S(1)} %fusion.4), custom_call_target="Cholesky" | custom-call | tf_op jit(solution)/shard_map/jit(cholesky)/cholesky | solution.py:24
  407.7 0.6 compare_reduce_fusion
  408.3 0.7 select_bitcast_fusion
  409.0 9.8 %custom-call.7 = f32[1,128,128]{1,2,0:T(8,128)S(1)} custom-call(f32[1,128,128]{2,1,0:T(8,128)S(1)} %get-tuple-element.3), custom_call_target="InvertDiagBlocksLowerTriangular" | custom-call | tf_op jit(solution)/shard_map/jit(_solve_triangular)/triangular_solve | solution.py:26
  418.8 0.2 fusion.2
  419.0 0.6 constant_dynamic-slice_fusion
  419.7 5.9 %fusion.5 = f32[8192,64]{0,1:T(8,128)} fusion(f32[8192,128]{0,1:T(8,128)} %all-gather.5.cloned.1.call-done, f32[128,128]{1,0:T(8,128)S(1)} %fusion.2, s32[]{:T(128)S(6)} %select_n.9), kind=kOutput, calls=%fused_computation.14 | convolution fusion | flops 805306368 | bytes 6324228 | tf_op jit(solution)/shard_map/fq,pq->fp/dot_general | solution.py:30
  425.6 0.0 copy-done.1
  425.6 0.7 copy.9
  (3 shorter events, 0.1 us)
Async XLA Ops:
  7.2 0.8 copy-start
  7.2 0.8 copy-start.2
  7.2 204.0 %all-gather.3.cloned.1.call-start = ((), (), s32[]{:S(2)}) async-start(), calls=%async_computation | async-start | bytes 25165824 | tf_op jit(solution)/shard_map/all_gather | solution.py:14
  7.9 271.5 %all-reduce.2.cloned.1.call-start = ((), (), s32[]{:S(2)}) async-start(), calls=%async_computation.1 | async-start | bytes 524288 | tf_op jit(solution)/shard_map/psum | solution.py:16
  224.3 130.7 %all-gather.5.cloned.1.call-start = ((), (), s32[]{:S(2)}) async-start(), calls=%async_computation.2 | async-start | bytes 6291456 | tf_op jit(solution)/shard_map/all_gather | solution.py:19
  362.3 63.3 %copy-start.1 = (f32[1024,64]{0,1:T(8,128)S(1)}, f32[1024,64]{0,1:T(8,128)}, u32[]{:S(2)}) copy-start(f32[1024,64]{0,1:T(8,128)} %all-reduce.2.cloned.1.call-done) | copy-start | bytes 786436
Sparse Core Ops, SparseCore 0:
  9.6 201.5 all-gather.2
  224.4 54.9 all-reduce.1
  299.3 55.7 all-gather.4
where the time goes:
time: 433 us
  waiting for transfers between devices  306 us (71%)
  matrix products  55 us (13%)
  blocking collectives  33.5 us (8%)
  other arithmetic  22.9 us (5%)
  between operations  13.8 us (3%)
    all_gather x1, waiting for transfers between devices, on_device(): lax.all_gather(basis, 'pts', axis=1, tiled=True).astype(jnp.float32)  194 us
    all_gather x1, waiting for transfers between devices, on_device(): spread = lax.all_gather(residual, 'pts', axis=1, tiled=True)  55.9 us
    psum x1, waiting for transfers between devices, on_device(): coefs = lax.psum(partial_value, ('feat', 'sub'))  54.8 us
    psum x1, blocking collectives, on_device(): block = lax.psum(block, ('feat', 'sub')) / FEATS  28.7 us
    dot_general x1, matrix products, on_device(): fitted = jnp.dot(whole_basis, coefs, precision=highest)  19.7 us
    dot_general x1, matrix products, on_device(): jnp.einsum('fk,fp->kp', whole_basis, features, precision=highest)  13.1 us
    another operation x3, other arithmetic, on_device(): factor = jnp.linalg.cholesky(gram)  12.4 us
    another operation x2, other arithmetic, on_device(): inverse = jax.scipy.linalg.solve_triangular(factor, eye_mat, lower=True)  10.5 us
  transfers between devices with their start and end apart: 3, of which 3 were waited for; matrix products, arithmetic and copies ran while one was open for 2% of the time, Pallas kernels for 0%

commit v1 on v0

--- a/solution.py
+++ b/solution.py
@@ -19,7 +19,7 @@
     spread = lax.all_gather(residual, "pts", axis=1, tiled=True)
     block = jnp.einsum("fq,fp->qp", spread, residual, precision=highest)
     total_pts = block.shape[0]
-    block = lax.psum(block, ("feat", "sub")) / FEATS
+    block = jnp.sum(lax.all_gather(block, ("feat", "sub")), axis=0) / FEATS
     gram = lax.all_gather(block, "pts", axis=1, tiled=True)
     factor = jnp.linalg.cholesky(gram)
     eye_mat = jnp.eye(total_pts, dtype=jnp.float32)

time: 433 us -> 419 us (0.968)
  blocking collectives: 33.5 us -> 19.2 us
    psum x1 -> x0, blocking collectives: 28.7 us -> none  [on_device(): block = lax.psum(block, ('feat', 'sub')) / FEATS]
    all_gather x0 -> x1, blocking collectives: none -> 14.4 us  [on_device(): block = jnp.sum(lax.all_gather(block, ('feat', 'sub')), axis=0) / FEATS]
where the time goes in v1:
time: 419 us
  waiting for transfers between devices  306 us (73%)
  matrix products  55 us (13%)
  other arithmetic  22.9 us (5%)
  blocking collectives  19.2 us (5%)
  between operations  13.8 us (3%)
    all_gather x1, waiting for transfers between devices, on_device(): lax.all_gather(basis, 'pts', axis=1, tiled=True).astype(jnp.float32)  194 us
    all_gather x1, waiting for transfers between devices, on_device(): spread = lax.all_gather(residual, 'pts', axis=1, tiled=True)  55.9 us
    psum x1, waiting for transfers between devices, on_device(): coefs = lax.psum(partial_value, ('feat', 'sub'))  54.8 us
    dot_general x1, matrix products, on_device(): fitted = jnp.dot(whole_basis, coefs, precision=highest)  19.7 us
    all_gather x1, blocking collectives, on_device(): block = jnp.sum(lax.all_gather(block, ('feat', 'sub')), axis=0) / FEATS  14.4 us
    dot_general x1, matrix products, on_device(): jnp.einsum('fk,fp->kp', whole_basis, features, precision=highest)  13.1 us
    another operation x3, other arithmetic, on_device(): factor = jnp.linalg.cholesky(gram)  12.4 us
    another operation x2, other arithmetic, on_device(): inverse = jax.scipy.linalg.solve_triangular(factor, eye_mat, lower=True)  10.5 us
  transfers between devices with their start and end apart: 3, of which 3 were waited for; matrix products, arithmetic and copies ran while one was open for 2% of the time, Pallas kernels for 0%

profile of v1, /device:TPU:0, one launch (start us, length us, event | category | flops | bytes accessed | tf_op | source)
XLA Modules:
  0.0 418.7 jit_solution(9225830552464086406)
XLA Ops:
  7.2 0.0 copy-start
  7.2 0.0 copy-start.2
  7.2 0.0 all-gather.4.cloned.1.call-start
  7.2 0.7 all-gather.4.cloned.1.call-update
  7.9 0.0 all-reduce.2.cloned.1.call-start
  8.0 0.0 copy-done
  8.0 0.0 copy-done.2
  8.0 8.7 %fusion = f32[8192,64]{0,1:T(8,128)S(1)} fusion(bf16[64,256]{1,0:T(8,128)(2,1)S(1)} %copy-done, bf16[256,8192]{1,0:T(8,128)(2,1)} %param.5, f32[8192]{0:T(1024)S(1)} %copy-done.2), kind=kOutput, calls=%fused_computation.1 | convolution fusion | flops 268959744 | bytes 6356992 | tf_op jit(solution)/shard_map/pd,df->fp/dot_general | solution.py:11
  16.7 194.4 %all-gather.4.cloned.1.call-done = bf16[8192,1024]{1,0:T(8,128)(2,1)} async-done(((bf16[8192,512]{1,0:T(8,128)(2,1)}), bf16[8192,1024]{1,0:T(8,128)(2,1)}) %all-gather.4.cloned.1.call-update) | async-done | bytes 16777232 | tf_op jit(solution)/shard_map/all_gather | solution.py:14
  211.2 13.1 %convolution_bitcast_fusion.1 = f32[1024,64]{0,1:T(8,128)} fusion(f32[8192,64]{0,1:T(8,128)S(1)} %fusion, bf16[8192,1024]{1,0:T(8,128)(2,1)} %all-gather.4.cloned.1.call-done), kind=kOutput, calls=%fused_computation.4 | convolution fusion | flops 6442450944 | bytes 19136512 | tf_op jit(solution)/shard_map/fk,fp->kp/dot_general | solution.py:15
  224.3 0.0 all-reduce.2.cloned.1.call-update
  224.3 0.2 all-gather.6.cloned.1.call-start
  224.5 54.8 %all-reduce.2.cloned.1.call-done = f32[1024,64]{0,1:T(8,128)} async-done(((f32[1024,64]{0,1:T(8,128)}), f32[1024,64]{0,1:T(8,128)}) %all-reduce.2.cloned.1.call-update) | async-done | bytes 262160 | tf_op jit(solution)/shard_map/psum | solution.py:16
  279.4 19.7 %fusion.1 = f32[8192,64]{0,1:T(8,128)} fusion(f32[8192,64]{0,1:T(8,128)S(1)} %fusion, f32[1024,64]{0,1:T(8,128)} %all-reduce.2.cloned.1.call-done, bf16[8192,1024]{1,0:T(8,128)(2,1)} %all-gather.4.cloned.1.call-done), kind=kOutput, calls=%fused_computation.3 | convolution fusion | flops 6442975232 | bytes 21233664 | tf_op jit(solution)/shard_map/dot_general | solution.py:17
  299.1 0.0 all-gather.6.cloned.1.call-update
  299.1 55.9 %all-gather.6.cloned.1.call-done = f32[8192,128]{0,1:T(8,128)} async-done(((f32[8192,64]{0,1:T(8,128)}), f32[8192,128]{0,1:T(8,128)}) %all-gather.6.cloned.1.call-update) | async-done | bytes 4194320 | tf_op jit(solution)/shard_map/all_gather | solution.py:19
  355.0 7.3 %fusion.8 = f32[128,64]{0,1:T(8,128)S(1)} fusion(f32[8192,128]{0,1:T(8,128)} %all-gather.6.cloned.1.call-done, f32[8192,64]{0,1:T(8,128)} %fusion.1), kind=kOutput, calls=%fused_computation.21 | convolution fusion | flops 805306368 | bytes 6324224 | tf_op jit(solution)/shard_map/fq,fp->qp/dot_general | solution.py:20
  362.3 0.0 copy-start.1
  362.3 14.4 %all-gather = f32[1024,64]{0,1:T(8,128)S(1)} all-gather(f32[128,64]{0,1:T(8,128)S(1)} %fusion.8), channel_id=2, replica_groups=mesh['groups'=2,'feat'=4,'pts'=2,'sub'=2] {'feat','sub'}, dimensions={0}, use_global_device_ids=true | all-gather | bytes 294912 | tf_op jit(solution)/shard_map/all_gather | solution.py:22
  376.7 0.1 bitcast_reduce_fusion
  376.8 4.8 %all_gather.19 = f32[128,128]{0,1:T(8,128)S(1)} all-gather(f32[128,64]{0,1:T(8,128)S(1)} %broadcast_multiply_fusion), channel_id=1, replica_groups=mesh['groups'=2,'feat'=4,'pts'=2,'sub'=2] {'pts'}, dimensions={1}, use_global_device_ids=true | all-gather | bytes 98304 | tf_op jit(solution)/shard_map/all_gather | solution.py:23
  381.6 0.1 copy.7
  381.7 11.7 %cholesky.17 = f32[128,128]{1,0:T(8,128)S(1)} custom-call(f32[128,128]{1,0:T(8,128)S(1)} %fusion.4), custom_call_target="Cholesky" | custom-call | tf_op jit(solution)/shard_map/jit(cholesky)/cholesky | solution.py:24
  393.5 0.6 compare_reduce_fusion
  394.1 0.7 select_bitcast_fusion
  394.8 9.8 %custom-call.7 = f32[1,128,128]{1,2,0:T(8,128)S(1)} custom-call(f32[1,128,128]{2,1,0:T(8,128)S(1)} %get-tuple-element.3), custom_call_target="InvertDiagBlocksLowerTriangular" | custom-call | tf_op jit(solution)/shard_map/jit(_solve_triangular)/triangular_solve | solution.py:26
  404.6 0.2 fusion.2
  404.9 0.6 constant_dynamic-slice_fusion
  405.5 5.9 %fusion.5 = f32[8192,64]{0,1:T(8,128)} fusion(f32[8192,128]{0,1:T(8,128)} %all-gather.6.cloned.1.call-done, f32[128,128]{1,0:T(8,128)S(1)} %fusion.2, s32[]{:T(128)S(6)} %select_n.9), kind=kOutput, calls=%fused_computation.15 | convolution fusion | flops 805306368 | bytes 6324228 | tf_op jit(solution)/shard_map/fq,pq->fp/dot_general | solution.py:30
  411.4 0.0 copy-done.1
  411.4 0.7 copy.10
  (4 shorter events, 0.1 us)
Async XLA Ops:
  7.2 0.8 copy-start
  7.2 0.8 copy-start.2
  7.2 204.0 %all-gather.4.cloned.1.call-start = ((), (), s32[]{:S(2)}) async-start(), calls=%async_computation | async-start | bytes 25165824 | tf_op jit(solution)/shard_map/all_gather | solution.py:14
  7.9 271.5 %all-reduce.2.cloned.1.call-start = ((), (), s32[]{:S(2)}) async-start(), calls=%async_computation.1 | async-start | bytes 524288 | tf_op jit(solution)/shard_map/psum | solution.py:16
  224.3 130.7 %all-gather.6.cloned.1.call-start = ((), (), s32[]{:S(2)}) async-start(), calls=%async_computation.2 | async-start | bytes 6291456 | tf_op jit(solution)/shard_map/all_gather | solution.py:19
  362.3 49.1 %copy-start.1 = (f32[1024,64]{0,1:T(8,128)S(1)}, f32[1024,64]{0,1:T(8,128)}, u32[]{:S(2)}) copy-start(f32[1024,64]{0,1:T(8,128)} %all-reduce.2.cloned.1.call-done) | copy-start | bytes 786436
Sparse Core Ops, SparseCore 0:
  9.6 201.5 all-gather.3
  224.4 54.9 all-reduce.1
  299.3 55.7 all-gather.5
